TPU v7x, 32 devices: a whole 2x2x4 slice. The times are simulated.
32 devices in a mesh: dp: 8 (over y, x, core), mp: 4 (over z).
Axes of the slice: x: 2, y: 2, z: 4, core: 2. Of those that a mesh axis runs over, the one named last changes fastest.
Arguments:
- tokens: bfloat16 [8192, 1536], P(('dp', 'mp')), may hold values from -6 to 6
- cotangent: bfloat16 [8192, 1536], P(('dp', 'mp')), may hold values from -6 to 6
- lengths: int32 [8, 8], P('dp'), may hold values from 1 to 512, 1024 in all within a row
- granularity: int32 [8], P('dp'), may hold values from 0 to 3
- ln1_gain: float32 [1536], replicated, may hold values from 0.5 to 1.5
- ln1_bias: float32 [1536], replicated, may hold values from -1.5 to 1.5
- w_qkv: bfloat16 [1536, 3, 1536], P('dp', None, 'mp'), may hold values from -0.21875 to 0.21875
- w_out: bfloat16 [1536, 1536], P(('mp', 'dp')), may hold values from -0.4375 to 0.4375
- ln2_gain: float32 [1536], replicated, may hold values from 0.5 to 1.5
- ln2_bias: float32 [1536], replicated, may hold values from -1.5 to 1.5
- w_up: bfloat16 [1536, 6144], P('dp', 'mp'), may hold values from -0.15625 to 0.15625
- w_down: bfloat16 [6144, 1536], P(('mp', 'dp')), may hold values from -0.15625 to 0.15625
Outputs:
- output: bfloat16 [8192, 1536], P(('dp', 'mp'))
- input_grad: bfloat16 [8192, 1536], P(('dp', 'mp'))
- grad_ln1_gain: float32 [1536], replicated
- grad_ln1_bias: float32 [1536], replicated
- grad_w_qkv: float32 [1536, 3, 1536], P('dp', None, 'mp')
- grad_w_out: float32 [1536, 1536], P(('mp', 'dp'))
- grad_ln2_gain: float32 [1536], replicated
- grad_ln2_bias: float32 [1536], replicated
- grad_w_up: float32 [1536, 6144], P('dp', 'mp')
- grad_w_down: float32 [6144, 1536], P(('mp', 'dp'))
Inputs may be any that keep to these rules, and one draw needn't show every extreme that they name: Row i lists the lengths of the 8 sequences packed in order into batch piece i; each row sums to 1024 and its longest sequence has exactly 512 tokens. Batch piece i uses the first 768 * 2^g hidden units of the feed-forward layer, g = granularity[i].
All inputs are finite; a program needn't handle non-finite values.
Results may differ from a plain program's by a relative error of at most 0.018.
Values may be sent and summed in bfloat16 or wider, within the bound.
No kernel may reach another device: no remote copies, remote signals or barrier semaphores. Data moves between devices by JAX's collectives and lax.ppermute only.
A program may use at most 128 MiB of HBM per device.

v0:
```python
import math
import jax
import jax.numpy as jnp
from jax import lax
from jax.sharding import PartitionSpec as P

HDIM = 128
PREFIX0 = 768
EPSILON = 1e-05
MASKED = -1e30


def piece_layout(seq_lengths, total_rows):
    seg_ends = jnp.cumsum(seq_lengths)
    starts = seg_ends - seq_lengths
    places = jnp.arange(total_rows, dtype=jnp.int32)
    seg_ids = jnp.sum((places[:, None] >= seg_ends[None, :]).astype(jnp.int32), axis=1)
    member = seg_ids[:, None] == jnp.arange(seq_lengths.shape[0], dtype=jnp.int32)[None, :]
    offsets = jnp.sum(jnp.where(member, starts[None, :], 0), axis=1)
    return (seg_ids, places - offsets)


def rotary_tables(positions, head_dim):
    half_dim = head_dim // 2
    frequencies = jnp.exp(
        jnp.arange(half_dim, dtype=jnp.float32) * (-2.0 * math.log(10000.0) / head_dim)
    )
    angles = positions.astype(jnp.float32)[:, None] * frequencies[None, :]
    return (jnp.cos(angles), jnp.sin(angles))


def rotate(values, cosine, sine):
    half_dim = values.shape[-1] // 2
    first_half = values[..., :half_dim]
    second_half = values[..., half_dim:]
    cos_rows = cosine[:, None, :]
    sin_rows = sine[:, None, :]
    return jnp.concatenate(
        [
            first_half * cos_rows - second_half * sin_rows,
            second_half * cos_rows + first_half * sin_rows,
        ],
        axis=-1,
    )


def norm_forward(values, norm_gain, norm_bias):
    center = values - jnp.mean(values, axis=-1, keepdims=True)
    inverse = lax.rsqrt(jnp.mean(center * center, axis=-1, keepdims=True) + EPSILON)
    normalized = center * inverse
    return (normalized * norm_gain + norm_bias, normalized, inverse)


def norm_backward(upstream, normalized, inverse, norm_gain):
    scaled = upstream * norm_gain
    return inverse * (
        scaled
        - jnp.mean(scaled, axis=-1, keepdims=True)
        - normalized * jnp.mean(scaled * normalized, axis=-1, keepdims=True)
    )


def gelu_back(pre_values, upstream):
    return jax.vjp(lambda pre_value: jax.nn.gelu(pre_value, approximate=True), pre_values)[1](
        upstream
    )[0]


def on_device(
    tokens,
    cotangent,
    lengths,
    granularity,
    ln1_gain,
    ln1_bias,
    w_qkv,
    w_out,
    ln2_gain,
    ln2_bias,
    w_up,
    w_down,
):
    mp_count = lax.axis_size("mp")
    mp_index = lax.axis_index("mp")
    wide_qkv, wide_up, wide_out, wide_down = (
        lax.all_gather(w_qkv, "dp", axis=0, tiled=True),
        lax.all_gather(w_up, "dp", axis=0, tiled=True),
        lax.all_gather(w_out, "dp", axis=0, tiled=True),
        lax.all_gather(w_down, "dp", axis=0, tiled=True),
    )
    local_rows = tokens.shape[0]
    total_rows = local_rows * mp_count
    head_width = wide_out.shape[0]
    local_heads = head_width // HDIM
    unit_count = wide_up.shape[1]
    block_rows = min(512, total_rows)
    block_count = total_rows // block_rows
    score_scale = HDIM ** (-0.5)
    seg_ids, positions = piece_layout(lengths[0], total_rows)
    places = jnp.arange(total_rows, dtype=jnp.int32)
    cosine, sine = rotary_tables(positions, HDIM)
    tokens_float = tokens.astype(jnp.float32)
    normed_one, unit_one, inverse_one = norm_forward(tokens_float, ln1_gain, ln1_bias)
    inputs_one = lax.all_gather(normed_one.astype(jnp.bfloat16), "mp", axis=0, tiled=True)
    projected = jnp.einsum("td,dch->tch", inputs_one, wide_qkv, preferred_element_type=jnp.float32)
    projected = projected.reshape(total_rows, 3, local_heads, HDIM)
    queries = rotate(projected[:, 0], cosine, sine).astype(jnp.bfloat16)
    keys_rot = rotate(projected[:, 1], cosine, sine).astype(jnp.bfloat16)
    values_all = projected[:, 2].astype(jnp.bfloat16)

    def block_scores(row_start):
        query_block = lax.dynamic_slice_in_dim(queries, row_start, block_rows, 0)
        seg_block = lax.dynamic_slice_in_dim(seg_ids, row_start, block_rows, 0)
        place_block = row_start + jnp.arange(block_rows, dtype=jnp.int32)
        scores = score_scale * jnp.einsum(
            "qhd,khd->hqk", query_block, keys_rot, preferred_element_type=jnp.float32
        )
        allowed = (seg_block[:, None] == seg_ids[None, :]) & (
            place_block[:, None] >= places[None, :]
        )
        return (jnp.where(allowed[None], scores, MASKED), query_block)

    def attend(block_index):
        scores, query_block = block_scores(block_index * block_rows)
        top_score = jnp.max(scores, axis=-1, keepdims=True)
        exp_scores = jnp.exp(scores - top_score)
        row_total = jnp.sum(exp_scores, axis=-1, keepdims=True)
        soft_weights = (exp_scores / row_total).astype(jnp.bfloat16)
        mixed_block = jnp.einsum(
            "hqk,khd->qhd", soft_weights, values_all, preferred_element_type=jnp.float32
        )
        return (mixed_block, (top_score + jnp.log(row_total))[..., 0])

    mixed_blocks, log_totals = lax.map(attend, jnp.arange(block_count, dtype=jnp.int32))
    mixed_heads = mixed_blocks.reshape(total_rows, head_width).astype(jnp.bfloat16)
    attn_part = jnp.dot(mixed_heads, wide_out, preferred_element_type=jnp.float32)
    resid_one = tokens_float + lax.psum_scatter(
        attn_part.astype(jnp.bfloat16), "mp", scatter_dimension=0, tiled=True
    ).astype(jnp.float32)
    normed_two, unit_two, inverse_two = norm_forward(resid_one, ln2_gain, ln2_bias)
    inputs_two = lax.all_gather(normed_two.astype(jnp.bfloat16), "mp", axis=0, tiled=True)
    prefix = PREFIX0 * jnp.left_shift(jnp.int32(1), granularity[0])
    active_units = jnp.clip(prefix - mp_index * unit_count, 0, unit_count)
    keep_units = (jnp.arange(unit_count, dtype=jnp.int32) < active_units).astype(jnp.float32)
    pre_act = jnp.dot(inputs_two, wide_up, preferred_element_type=jnp.float32)
    hidden_act = (jax.nn.gelu(pre_act, approximate=True) * keep_units).astype(jnp.bfloat16)
    ffn_part = jnp.dot(hidden_act, wide_down, preferred_element_type=jnp.float32)
    output = (
        resid_one
        + lax.psum_scatter(
            ffn_part.astype(jnp.bfloat16), "mp", scatter_dimension=0, tiled=True
        ).astype(jnp.float32)
    ).astype(jnp.bfloat16)
    cot_all = lax.all_gather(cotangent, "mp", axis=0, tiled=True)
    hidden_grad = jnp.einsum("td,sd->ts", cot_all, wide_down, preferred_element_type=jnp.float32)
    pre_grad = (gelu_back(pre_act, hidden_grad) * keep_units).astype(jnp.bfloat16)
    grad_up = jnp.einsum("td,ts->ds", inputs_two, pre_grad, preferred_element_type=jnp.float32)
    grad_down = jnp.einsum("ts,td->sd", hidden_act, cot_all, preferred_element_type=jnp.float32)
    ffn_back_part = jnp.einsum("ts,ds->td", pre_grad, wide_up, preferred_element_type=jnp.float32)
    normed_two_grad = lax.psum_scatter(
        ffn_back_part.astype(jnp.bfloat16), "mp", scatter_dimension=0, tiled=True
    ).astype(jnp.float32)
    resid_grad = cotangent.astype(jnp.float32) + norm_backward(
        normed_two_grad, unit_two, inverse_two, ln2_gain
    )
    gain_two_grad = jnp.sum(normed_two_grad * unit_two, axis=0)
    bias_two_grad = jnp.sum(normed_two_grad, axis=0)
    resid_all = lax.all_gather(resid_grad.astype(jnp.bfloat16), "mp", axis=0, tiled=True)
    grad_out = jnp.einsum("th,td->hd", mixed_heads, resid_all, preferred_element_type=jnp.float32)
    mixed_grad = jnp.einsum(
        "td,hd->th", resid_all, wide_out, preferred_element_type=jnp.float32
    ).astype(jnp.bfloat16)
    mixed_grad = mixed_grad.reshape(total_rows, local_heads, HDIM)

    def attend_back(running, block_index):
        key_sum, value_sum = running
        row_start = block_index * block_rows
        scores, query_block = block_scores(row_start)
        log_block = lax.dynamic_index_in_dim(log_totals, block_index, 0, keepdims=False)
        soft_float = jnp.exp(scores - log_block[..., None])
        grad_block = lax.dynamic_slice_in_dim(mixed_grad, row_start, block_rows, 0)
        prob_grad = jnp.einsum(
            "qhd,khd->hqk", grad_block, values_all, preferred_element_type=jnp.float32
        )
        score_grad = (
            soft_float * (prob_grad - jnp.sum(soft_float * prob_grad, axis=-1, keepdims=True))
        ).astype(jnp.bfloat16)
        query_grad = score_scale * jnp.einsum(
            "hqk,khd->qhd", score_grad, keys_rot, preferred_element_type=jnp.float32
        )
        key_sum = key_sum + score_scale * jnp.einsum(
            "hqk,qhd->khd", score_grad, query_block, preferred_element_type=jnp.float32
        )
        value_sum = value_sum + jnp.einsum(
            "hqk,qhd->khd",
            soft_float.astype(jnp.bfloat16),
            grad_block,
            preferred_element_type=jnp.float32,
        )
        return ((key_sum, value_sum), query_grad)

    zero_heads = jnp.zeros((total_rows, local_heads, HDIM), jnp.float32)
    (key_grad, value_grad), query_grads = lax.scan(
        attend_back, (zero_heads, zero_heads), jnp.arange(block_count, dtype=jnp.int32)
    )
    query_grad_all = query_grads.reshape(total_rows, local_heads, HDIM)
    projected_grad = jnp.stack(
        [
            rotate(query_grad_all, cosine, -sine).reshape(total_rows, head_width),
            rotate(key_grad, cosine, -sine).reshape(total_rows, head_width),
            value_grad.reshape(total_rows, head_width),
        ],
        axis=1,
    ).astype(jnp.bfloat16)
    grad_qkv = jnp.einsum(
        "td,tch->dch", inputs_one, projected_grad, preferred_element_type=jnp.float32
    )
    attn_back_part = jnp.einsum(
        "tch,dch->td", projected_grad, wide_qkv, preferred_element_type=jnp.float32
    )
    normed_one_grad = lax.psum_scatter(
        attn_back_part.astype(jnp.bfloat16), "mp", scatter_dimension=0, tiled=True
    ).astype(jnp.float32)
    input_grad = (
        resid_grad + norm_backward(normed_one_grad, unit_one, inverse_one, ln1_gain)
    ).astype(jnp.bfloat16)
    gain_one_grad = jnp.sum(normed_one_grad * unit_one, axis=0)
    bias_one_grad = jnp.sum(normed_one_grad, axis=0)
    norm_sums = lax.psum((gain_one_grad, bias_one_grad, gain_two_grad, bias_two_grad), ("dp", "mp"))
    grad_qkv_shard, grad_up_shard, grad_out_shard, grad_down_shard = (
        lax.psum_scatter(grad_qkv, "dp", scatter_dimension=0, tiled=True),
        lax.psum_scatter(grad_up, "dp", scatter_dimension=0, tiled=True),
        lax.psum_scatter(grad_out, "dp", scatter_dimension=0, tiled=True),
        lax.psum_scatter(grad_down, "dp", scatter_dimension=0, tiled=True),
    )
    return (
        output,
        input_grad,
        norm_sums[0],
        norm_sums[1],
        grad_qkv_shard,
        grad_out_shard,
        norm_sums[2],
        norm_sums[3],
        grad_up_shard,
        grad_down_shard,
    )


def solution(mesh):
    return jax.shard_map(
        on_device,
        mesh=mesh,
        in_specs=(
            P(("dp", "mp"), None),
            P(("dp", "mp"), None),
            P("dp", None),
            P("dp"),
            P(),
            P(),
            P("dp", None, "mp"),
            P(("mp", "dp"), None),
            P(),
            P(),
            P("dp", "mp"),
            P(("mp", "dp"), None),
        ),
        out_specs=(
            P(("dp", "mp"), None),
            P(("dp", "mp"), None),
            P(),
            P(),
            P("dp", None, "mp"),
            P(("mp", "dp"), None),
            P(),
            P(),
            P("dp", "mp"),
            P(("mp", "dp"), None),
        ),
        check_vma=False,
    )
```

profile of v0, /device:TPU:0, one launch (start us, length us, event | category | flops | bytes accessed | tf_op | source)
XLA Modules:
  0.0 1039.5 jit_solution(4531013267683974176)
XLA Ops:
  17.6 61.3 %all-gather.9.cloned.1.call-done = bf16[1024,1536]{1,0:T(8,128)(2,1)} async-done(((bf16[256,1536]{1,0:T(8,128)(2,1)}), bf16[1024,1536]{1,0:T(8,128)(2,1)}) %all-gather.9.cloned.1.call-update) | async-done | bytes 3145744 | tf_op jit(solution)/shard_map/all_gather | solution.py:104
  78.9 34.6 %all-gather.11.cloned.1.call-done = bf16[1536,3,384]{2,0,1:T(8,128)(2,1)} async-done(((bf16[192,3,384]{2,0,1:T(8,128)(2,1)}), bf16[1536,3,384]{2,0,1:T(8,128)(2,1)}) %all-gather.11.cloned.1.call-update) | async-done | bytes 3538960 | tf_op jit(solution)/shard_map/all_gather | solution.py:86
  132.0 15.6 %while.28 = (s32[]{:T(128)}, bf16[2,512,3,128]{3,1,2,0:T(8,128)(2,1)S(1)}, f32[2,3,512]{2,1,0:T(4,128)S(1)}, s32[2]{0:T(128)S(1)}, s32[1024]{0:T(1024)S(1)}, /*i...) while((s32[]{:T(128)}, ...), condition=%wide.region_8.9_spmd.clone, body=%wide.region_5.8_spmd.clone.sunk | while | flops 825752576 | bytes 23797964 | solution.py:134
  159.3 58.4 %reduce-scatter.9.cloned.1.call-done = bf16[256,1536]{1,0:T(8,128)(2,1)} async-done(((bf16[1024,1536]{1,0:T(8,128)(2,1)}), bf16[256,1536]{1,0:T(8,128)(2,1)}) %reduce-scatter.9.cloned.1.call-update) | async-done | bytes 786448 | tf_op jit(solution)/shard_map/reduce_scatter | solution.py:137
  222.8 59.9 %all-gather.21.cloned.1.call-done = bf16[1024,1536]{1,0:T(8,128)(2,1)} async-done(((bf16[256,1536]{1,0:T(8,128)(2,1)}), bf16[1024,1536]{1,0:T(8,128)(2,1)}) %all-gather.21.cloned.1.call-update) | async-done | bytes 3145744 | tf_op jit(solution)/shard_map/all_gather | solution.py:154
  282.7 39.3 %all-gather.19.cloned.1.call-done = bf16[1536,1536]{1,0:T(8,128)(2,1)} async-done(((bf16[192,1536]{1,0:T(8,128)(2,1)}), bf16[1536,1536]{1,0:T(8,128)(2,1)}) %all-gather.19.cloned.1.call-update) | async-done | bytes 4718608 | tf_op jit(solution)/shard_map/all_gather | solution.py:89
  322.0 9.8 fusion.84
  331.8 31.1 %all-gather.17.cloned.1.call-done = bf16[1536,1536]{1,0:T(8,128)(2,1)} async-done(((bf16[192,1536]{1,0:T(8,128)(2,1)}), bf16[1536,1536]{1,0:T(8,128)(2,1)}) %all-gather.17.cloned.1.call-update) | async-done | bytes 4718608 | tf_op jit(solution)/shard_map/all_gather | solution.py:87
  362.9 65.7 %all-gather.15.cloned.1.call-done = bf16[1024,1536]{1,0:T(8,128)(2,1)} async-done(((bf16[256,1536]{1,0:T(8,128)(2,1)}), bf16[1024,1536]{1,0:T(8,128)(2,1)}) %all-gather.15.cloned.1.call-update) | async-done | bytes 3145744 | tf_op jit(solution)/shard_map/all_gather | solution.py:141
  428.6 13.7 %fusion.46 = (bf16[1024,1536]{1,0:T(8,128)(2,1)S(1)}, f32[1024,1536]{1,0:T(8,128)}) fusion(f32[1024,1536]{1,0:T(8,128)} %fusion.84, f32[1536]{0:T(1024)S(1)} %fusion.77, bf16[1024,1536]{1,0:T(8,128)(2,1)} %all-gather.15.cloned.1.call-done, bf16[1536,1536]{1,0:T(8,128)(2,1)} %all-gather.17.cloned.1.call-done), kind=kOutput, calls=%fused_computation.58 | convolution fusion | flops 4864868352 | bytes 23599104 | tf_op jit(solution)/shard_map/dot_general | solution.py:145
  450.5 59.0 %reduce-scatter.13.cloned.1.call-done = bf16[256,1536]{1,0:T(8,128)(2,1)} async-done(((bf16[1024,1536]{1,0:T(8,128)(2,1)}), bf16[256,1536]{1,0:T(8,128)(2,1)}) %reduce-scatter.13.cloned.1.call-update) | async-done | bytes 786448 | tf_op jit(solution)/shard_map/reduce_scatter | solution.py:160
  514.3 63.4 %all-gather.23.cloned.1.call-done = bf16[1024,1536]{1,0:T(8,128)(2,1)} async-done(((bf16[256,1536]{1,0:T(8,128)(2,1)}), bf16[1024,1536]{1,0:T(8,128)(2,1)}) %all-gather.23.cloned.1.call-update) | async-done | bytes 3145744 | tf_op jit(solution)/shard_map/all_gather | solution.py:168
  582.2 32.5 %while.29 = (s32[]{:T(128)}, f32[1024,3,128]{0,2,1:T(8,128)S(1)}, f32[1024,3,128]{0,2,1:T(8,128)}, f32[2,512,3,128]{3,1,0,2:T(8,128)}, s32[2]{0:T(128)S(1)}, /*i...) while((s32[]{:T(128)}, f32[1024,3,128]{0,2,1:T(8,128)S(1)}, ...), condition=%wide.region_18.19_spmd.clone, body=%wide.region_16.18_spmd.clone.sunk | while | flops 2040593408 | bytes 91812304 | solution.py:203
  632.8 10.3 convolution_convert_fusion.1
  643.1 10.1 fusion.86
  653.3 11.0 %fusion.82 = f32[1536,1536]{1,0:T(8,128)} fusion(bf16[1024,1536]{1,0:T(8,128)(2,1)} %all-gather.21.cloned.1.call-done, f32[1024,1536]{1,0:T(8,128)} %get-tuple-element.298, f32[1536]{0:T(1024)S(1)} %fusion.77), kind=kOutput, calls=%fused_computation.145 | convolution fusion | flops 4847566848 | bytes 18880512 | tf_op jit(solution)/shard_map/ts,td->sd/dot_general | solution.py:158
  670.5 9.1 fusion.47
  679.7 12.1 %reduce-scatter.15.cloned.1.call-done = bf16[256,1536]{1,0:T(8,128)(2,1)} async-done(((bf16[1024,1536]{1,0:T(8,128)(2,1)}), bf16[256,1536]{1,0:T(8,128)(2,1)}) %reduce-scatter.15.cloned.1.call-update) | async-done | bytes 786448 | tf_op jit(solution)/shard_map/reduce_scatter | solution.py:221
  693.8 45.5 %all-reduce = (f32[1536]{0:T(1024)}, f32[1536]{0:T(1024)}, f32[1536]{0:T(1024)}, f32[1536]{0:T(1024)}) all-reduce(f32[1536]{0:T(1024)S(1)} %get-tuple-element.226, f32[1536]{0:T(1024)S(1)} %get-tuple-element.231, f32[1536]{0:T(1024)S(1)} %copy-done.27, f32[1536]{0:T(1024)S(1)} %copy-done.28), channel_id=1, replica_groups=mesh['dp'=8,'mp'=4] {'dp','mp'}, use_global_device_ids=true, to_apply=%region_23.24 | all-reduce | flops 6144 | bytes 49152 | tf_op jit(solution)/shard_map/psum | solution.py:229
  739.3 16.0 %reduce-scatter.11.cloned.1.call-done = bf16[256,1536]{1,0:T(8,128)(2,1)} async-done(((bf16[1024,1536]{1,0:T(8,128)(2,1)}), bf16[256,1536]{1,0:T(8,128)(2,1)}) %reduce-scatter.11.cloned.1.call-update) | async-done | bytes 786448 | tf_op jit(solution)/shard_map/reduce_scatter | solution.py:150
  759.0 77.0 %reduce-scatter.21.cloned.1.call-done = f32[192,1536]{1,0:T(8,128)} async-done(((f32[1536,1536]{1,0:T(8,128)}), f32[192,1536]{1,0:T(8,128)}) %reduce-scatter.21.cloned.1.call-update) | async-done | bytes 1179664 | tf_op jit(solution)/shard_map/reduce_scatter | solution.py:232
  836.0 80.4 %reduce-scatter.23.cloned.1.call-done = f32[192,1536]{1,0:T(8,128)} async-done(((f32[1536,1536]{1,0:T(8,128)}), f32[192,1536]{1,0:T(8,128)}) %reduce-scatter.23.cloned.1.call-update) | async-done | bytes 1179664 | tf_op jit(solution)/shard_map/reduce_scatter | solution.py:234
  916.4 46.3 %reduce-scatter.19.cloned.1.call-done = f32[48,1536]{1,0:T(8,128)} async-done(((f32[384,1536]{1,0:T(8,128)}), f32[48,1536]{1,0:T(8,128)}) %reduce-scatter.19.cloned.1.call-update) | async-done | bytes 294928 | tf_op jit(solution)/shard_map/reduce_scatter | solution.py:233
  962.7 69.9 %reduce-scatter.17.cloned.1.call-done = f32[192,3,384]{2,0,1:T(8,128)} async-done(((f32[1536,3,384]{2,0,1:T(8,128)}), f32[192,3,384]{2,0,1:T(8,128)}) %reduce-scatter.17.cloned.1.call-update) | async-done | bytes 884752 | tf_op jit(solution)/shard_map/reduce_scatter | solution.py:231
  (227 shorter events, 133.6 us)
Async XLA Ops:
  7.2 71.7 %all-gather.9.cloned.1.call-start = ((), (), s32[]{:S(2)}) async-start(), calls=%async_computation.8 | async-start | bytes 3932160 | tf_op jit(solution)/shard_map/all_gather | solution.py:104
  10.1 110.3 %copy-start.33 = (f32[256]{0:T(256)}, f32[256]{0:T(256)S(1)}, u32[]{:S(2)}) copy-start(f32[256]{0:T(256)S(1)} %add_rsqrt_fusion.1) | copy-start | bytes 3076
  12.5 100.9 %all-gather.11.cloned.1.call-start = ((), (), s32[]{:S(2)}) async-start(), calls=%async_computation.9 | async-start | bytes 3981312 | tf_op jit(solution)/shard_map/all_gather | solution.py:86
  13.2 139.1 %all-gather.13.cloned.1.call-start = ((), (), s32[]{:S(2)}) async-start(), calls=%async_computation.10 | async-start | bytes 1327104 | tf_op jit(solution)/shard_map/all_gather | solution.py:88
  14.0 203.7 %reduce-scatter.9.cloned.1.call-start = ((), (), s32[]{:S(2)}) async-start(), calls=%async_computation.11 | async-start | bytes 3932160 | tf_op jit(solution)/shard_map/reduce_scatter | solution.py:137
  157.3 125.4 %all-gather.21.cloned.1.call-start = ((), (), s32[]{:S(2)}) async-start(), calls=%async_computation.16 | async-start | bytes 3932160 | tf_op jit(solution)/shard_map/all_gather | solution.py:154
  157.9 164.1 %all-gather.19.cloned.1.call-start = ((), (), s32[]{:S(2)}) async-start(), calls=%async_computation.14 | async-start | bytes 5308416 | tf_op jit(solution)/shard_map/all_gather | solution.py:89
  158.5 204.4 %all-gather.17.cloned.1.call-start = ((), (), s32[]{:S(2)}) async-start(), calls=%async_computation.13 | async-start | bytes 5308416 | tf_op jit(solution)/shard_map/all_gather | solution.py:87
  159.2 269.3 %all-gather.15.cloned.1.call-start = ((), (), s32[]{:S(2)}) async-start(), calls=%async_computation.12 | async-start | bytes 3932160 | tf_op jit(solution)/shard_map/all_gather | solution.py:141
  219.2 293.0 %copy-start.25 = (f32[256]{0:T(256)}, f32[256]{0:T(256)S(1)}, u32[]{:S(2)}) copy-start(f32[256]{0:T(256)S(1)} %broadcast_multiply_fusion.4) | copy-start | bytes 3076
  220.8 291.4 %copy-start.31 = (f32[256]{0:T(256)}, f32[256]{0:T(256)S(1)}, u32[]{:S(2)}) copy-start(f32[256]{0:T(256)S(1)} %add_rsqrt_fusion) | copy-start | bytes 3076
  222.1 287.4 %reduce-scatter.13.cloned.1.call-start = ((), (), s32[]{:S(2)}) async-start(), calls=%async_computation.17 | async-start | bytes 3932160 | tf_op jit(solution)/shard_map/reduce_scatter | solution.py:160
  450.4 127.3 %all-gather.23.cloned.1.call-start = ((), (), s32[]{:S(2)}) async-start(), calls=%async_computation.18 | async-start | bytes 3932160 | tf_op jit(solution)/shard_map/all_gather | solution.py:168
  514.1 177.8 %reduce-scatter.15.cloned.1.call-start = ((), (), s32[]{:S(2)}) async-start(), calls=%async_computation.19 | async-start | bytes 3932160 | tf_op jit(solution)/shard_map/reduce_scatter | solution.py:221
  632.8 122.5 %reduce-scatter.11.cloned.1.call-start = ((), (), s32[]{:S(2)}) async-start(), calls=%async_computation.15 | async-start | bytes 3932160 | tf_op jit(solution)/shard_map/reduce_scatter | solution.py:150
  643.1 192.9 %reduce-scatter.21.cloned.1.call-start = ((), (), s32[]{:S(2)}) async-start(), calls=%async_computation.22 | async-start | bytes 10616832 | tf_op jit(solution)/shard_map/reduce_scatter | solution.py:232
  653.3 263.1 %reduce-scatter.23.cloned.1.call-start = ((), (), s32[]{:S(2)}) async-start(), calls=%async_computation.23 | async-start | bytes 10616832 | tf_op jit(solution)/shard_map/reduce_scatter | solution.py:234
  664.3 298.3 %reduce-scatter.19.cloned.1.call-start = ((), (), s32[]{:S(2)}) async-start(), calls=%async_computation.21 | async-start | bytes 2654208 | tf_op jit(solution)/shard_map/reduce_scatter | solution.py:233
  670.1 362.4 %reduce-scatter.17.cloned.1.call-start = ((), (), s32[]{:S(2)}) async-start(), calls=%async_computation.20 | async-start | bytes 7962624 | tf_op jit(solution)/shard_map/reduce_scatter | solution.py:231
  679.6 75.7 %copy-start.5 = (bf16[256,1536]{1,0:T(8,128)(2,1)S(1)}, bf16[256,1536]{1,0:T(8,128)(2,1)}, u32[]{:S(2)}) copy-start(bf16[256,1536]{1,0:T(8,128)(2,1)} %reduce-scatter.9.cloned.1.call-done) | copy-start | bytes 2359300
  679.6 75.7 %copy-start.7 = (bf16[256,1536]{1,0:T(8,128)(2,1)S(1)}, bf16[256,1536]{1,0:T(8,128)(2,1)}, u32[]{:S(2)}) copy-start(bf16[256,1536]{1,0:T(8,128)(2,1)} %param.17) | copy-start | bytes 2359300
  679.6 75.7 %copy-start.9 = (bf16[256,1536]{1,0:T(8,128)(2,1)S(1)}, bf16[256,1536]{1,0:T(8,128)(2,1)}, u32[]{:S(2)}) copy-start(bf16[256,1536]{1,0:T(8,128)(2,1)} %reduce-scatter.13.cloned.1.call-done) | copy-start | bytes 2359300
  679.6 75.7 %copy-start.23 = (f32[1536]{0:T(1024)S(1)}, f32[1536]{0:T(1024)}, u32[]{:S(2)}) copy-start(f32[1536]{0:T(1024)} %param.24) | copy-start | bytes 18436
  679.6 75.7 %copy-start.26 = (f32[256]{0:T(256)S(1)}, f32[256]{0:T(256)}, u32[]{:S(2)}) copy-start(f32[256]{0:T(256)} %copy-done.25) | copy-start | bytes 3076
  (41 other events, 581.1 us)
Sparse Core Ops, SparseCore 0:
  12.6 66.1 all-gather.8
  80.7 32.6 all-gather.10
  115.3 24.0 all-gather.12
  157.4 60.2 reduce-scatter.8
  219.1 63.5 all-gather.20
  284.4 37.5 all-gather.18
  323.9 38.9 all-gather.16
  365.0 63.4 all-gather.14
  450.5 58.8 reduce-scatter.12
  514.2 63.5 all-gather.22
  632.9 58.8 reduce-scatter.14
  694.0 61.2 reduce-scatter.10
  759.4 76.5 reduce-scatter.20
  839.9 76.4 reduce-scatter.22
  920.2 42.4 reduce-scatter.18
  967.0 65.4 reduce-scatter.16
where the time goes:
time: 1050 us; the launch traced here: 1040 us
  waiting for transfers between devices  778 us (74%)
  matrix products  124 us (12%)
  blocking collectives  45.5 us (4%)
  other arithmetic  42.5 us (4%)
  local copies, waits for them, and re-layouts  26.7 us (3%)
  between operations  15.6 us (1%)
    reduce_scatter x1, waiting for transfers between devices, on_device(): lax.psum_scatter(grad_down, 'dp', scatter_dimension=0, tiled=True)  80.4 us
    reduce_scatter x1, waiting for transfers between devices, on_device(): lax.psum_scatter(grad_up, 'dp', scatter_dimension=0, tiled=True)  77 us
    reduce_scatter x1, waiting for transfers between devices, on_device(): lax.psum_scatter(grad_qkv, 'dp', scatter_dimension=0, tiled=True)  69.9 us
    all_gather x1, waiting for transfers between devices, on_device(): lax.all_gather(normed_two.astype(jnp.bfloat16), 'mp', axis=0, tiled=True)  65.7 us
    all_gather x1, waiting for transfers between devices, on_device(): lax.all_gather(resid_grad.astype(jnp.bfloat16), 'mp', axis=0, tiled=True)  63.4 us
    all_gather x1, waiting for transfers between devices, on_device(): lax.all_gather(normed_one.astype(jnp.bfloat16), 'mp', axis=0, tiled=True)  61.3 us
    all_gather x1, waiting for transfers between devices, on_device(): cot_all = lax.all_gather(cotangent, 'mp', axis=0, tiled=True)  59.9 us
    reduce_scatter x1, waiting for transfers between devices, on_device(): lax.psum_scatter(ffn_back_part.astype(jnp.bfloat16), 'mp', scatter_dimens...  59 us
  transfers between devices with their start and end apart: 16, of which 15 were waited for; matrix products, arithmetic and copies ran while one was open for 10% of the time, Pallas kernels for 0%

commit v1 on v0

--- a/solution.py
+++ b/solution.py
@@ -151,7 +151,12 @@
             ffn_part.astype(jnp.bfloat16), "mp", scatter_dimension=0, tiled=True
         ).astype(jnp.float32)
     ).astype(jnp.bfloat16)
-    cot_all = lax.all_gather(cotangent, "mp", axis=0, tiled=True)
+    ring = [cotangent]
+    for hop in range(3):
+        ring.append(lax.ppermute(ring[-1], "mp", [(dev, (dev + 1) % 4) for dev in range(4)]))
+    cot_all = jnp.roll(
+        jnp.concatenate(ring[::-1], axis=0), (lax.axis_index("mp") + 1) * ring[0].shape[0], axis=0
+    )
     hidden_grad = jnp.einsum("td,sd->ts", cot_all, wide_down, preferred_element_type=jnp.float32)
     pre_grad = (gelu_back(pre_act, hidden_grad) * keep_units).astype(jnp.bfloat16)
     grad_up = jnp.einsum("td,ts->ds", inputs_two, pre_grad, preferred_element_type=jnp.float32)

time: 1050 us -> 997 us (0.950)
  waiting for transfers between devices: 778 us -> 711 us
  local copies, waits for them, and re-layouts: 26.7 us -> 39.2 us
    ppermute x0 -> x3, waiting for transfers between devices: none -> 73.5 us  [on_device(): lax.ppermute(ring[-1], 'mp', [(dev, (dev + 1) % 4) for dev in range(4)])]
    all_gather x1 -> x0, waiting for transfers between devices: 59.9 us -> none  [on_device(): cot_all = lax.all_gather(cotangent, 'mp', axis=0, tiled=True)]
    all_gather x1, waiting for transfers between devices: 65.7 us -> 24.5 us  [on_device(): lax.all_gather(normed_two.astype(jnp.bfloat16), 'mp', axis=0, tiled=True)]
    all_gather x1, waiting for transfers between devices: 31.1 us -> 0.01 us  [on_device(): lax.all_gather(w_up, 'dp', axis=0, tiled=True)]
    unnamed x78 -> x87, local copies, waits for them, and re-layouts: 10.8 us -> 22.5 us
  transfers between devices with their start and end apart: 16 -> 18, of which waited for: 15 -> 16; matrix products, arithmetic and copies ran while one was open for 10% -> 12% of each run, Pallas kernels for 0% -> 0%
where the time goes in v1:
time: 997 us; the launch traced here: 987 us
  waiting for transfers between devices  711 us (71%)
  matrix products  123 us (12%)
  blocking collectives  45.7 us (5%)
  other arithmetic  43.7 us (4%)
  local copies, waits for them, and re-layouts  39.2 us (4%)
  between operations  15.4 us (2%)
    reduce_scatter x1, waiting for transfers between devices, on_device(): lax.psum_scatter(grad_up, 'dp', scatter_dimension=0, tiled=True)  80.6 us
    reduce_scatter x1, waiting for transfers between devices, on_device(): lax.psum_scatter(grad_down, 'dp', scatter_dimension=0, tiled=True)  76.8 us
    ppermute x3, waiting for transfers between devices, on_device(): lax.ppermute(ring[-1], 'mp', [(dev, (dev + 1) % 4) for dev in range(4)])  73.5 us
    reduce_scatter x1, waiting for transfers between devices, on_device(): lax.psum_scatter(grad_qkv, 'dp', scatter_dimension=0, tiled=True)  69.9 us
    all_gather x1, waiting for transfers between devices, on_device(): lax.all_gather(resid_grad.astype(jnp.bfloat16), 'mp', axis=0, tiled=True)  63.4 us
    all_gather x1, waiting for transfers between devices, on_device(): lax.all_gather(normed_one.astype(jnp.bfloat16), 'mp', axis=0, tiled=True)  61.3 us
    reduce_scatter x1, waiting for transfers between devices, on_device(): lax.psum_scatter(ffn_back_part.astype(jnp.bfloat16), 'mp', scatter_dimens...  60.4 us
    reduce_scatter x1, waiting for transfers between devices, on_device(): lax.psum_scatter(attn_part.astype(jnp.bfloat16), 'mp', scatter_dimension=...  59.8 us
  transfers between devices with their start and end apart: 18, of which 16 were waited for; matrix products, arithmetic and copies ran while one was open for 12% of the time, Pallas kernels for 0%

profile of v1, /device:TPU:0, one launch (start us, length us, event | category | flops | bytes accessed | tf_op | source)
XLA Modules:
  0.0 986.9 jit_solution(18360328964080986529)
XLA Ops:
  17.6 61.3 %all-gather.8.cloned.1.call-done = bf16[1024,1536]{1,0:T(8,128)(2,1)} async-done(((bf16[256,1536]{1,0:T(8,128)(2,1)}), bf16[1024,1536]{1,0:T(8,128)(2,1)}) %all-gather.8.cloned.1.call-update) | async-done | bytes 3145744 | tf_op jit(solution)/shard_map/all_gather | solution.py:104
  78.9 34.6 %all-gather.10.cloned.1.call-done = bf16[1536,3,384]{2,0,1:T(8,128)(2,1)} async-done(((bf16[192,3,384]{2,0,1:T(8,128)(2,1)}), bf16[1536,3,384]{2,0,1:T(8,128)(2,1)}) %all-gather.10.cloned.1.call-update) | async-done | bytes 3538960 | tf_op jit(solution)/shard_map/all_gather | solution.py:86
  132.0 15.6 %while.28 = (s32[]{:T(128)}, bf16[2,512,3,128]{3,1,2,0:T(8,128)(2,1)S(1)}, f32[2,3,512]{2,1,0:T(4,128)S(1)}, s32[2]{0:T(128)S(1)}, s32[1024]{0:T(1024)S(1)}, /*i...) while((s32[]{:T(128)}, ...), condition=%wide.region_8.9_spmd.clone, body=%wide.region_5.8_spmd.clone.sunk | while | flops 825752576 | bytes 23797964 | solution.py:134
  157.8 59.8 %reduce-scatter.9.cloned.1.call-done = bf16[256,1536]{1,0:T(8,128)(2,1)} async-done(((bf16[1024,1536]{1,0:T(8,128)(2,1)}), bf16[256,1536]{1,0:T(8,128)(2,1)}) %reduce-scatter.9.cloned.1.call-update) | async-done | bytes 786448 | tf_op jit(solution)/shard_map/reduce_scatter | solution.py:137
  223.8 20.1 %collective-permute-done = bf16[256,1536]{1,0:T(8,128)(2,1)S(1)} collective-permute-done((bf16[256,1536]{1,0:T(8,128)(2,1)}, bf16[256,1536]{1,0:T(8,128)(2,1)S(1)}, u32[]{:S(2)}, u32[]{:S(2)}) %collective-permute-start) | collective-permute-done | bytes 786464 | tf_op jit(solution)/shard_map/ppermute | solution.py:156
  244.8 20.1 %collective-permute-done.1 = bf16[256,1536]{1,0:T(8,128)(2,1)} collective-permute-done((bf16[256,1536]{1,0:T(8,128)(2,1)S(1)}, bf16[256,1536]{1,0:T(8,128)(2,1)}, u32[]{:S(2)}, u32[]{:S(2)}) %collective-permute-start.1) | collective-permute-done | bytes 786464 | tf_op jit(solution)/shard_map/ppermute | solution.py:156
  265.7 33.3 %collective-permute-done.2 = bf16[256,1536]{1,0:T(8,128)(2,1)} collective-permute-done((bf16[256,1536]{1,0:T(8,128)(2,1)}, bf16[256,1536]{1,0:T(8,128)(2,1)}, u32[]{:S(2)}, u32[]{:S(2)}) %collective-permute-start.2) | collective-permute-done | bytes 786464 | tf_op jit(solution)/shard_map/ppermute | solution.py:156
  311.0 24.5 %all-gather.14.cloned.1.call-done = bf16[1024,1536]{1,0:T(8,128)(2,1)} async-done(((bf16[256,1536]{1,0:T(8,128)(2,1)}), bf16[1024,1536]{1,0:T(8,128)(2,1)}) %all-gather.14.cloned.1.call-update) | async-done | bytes 3145744 | tf_op jit(solution)/shard_map/all_gather | solution.py:141
  335.6 9.7 fusion.91
  345.2 29.4 %all-gather.18.cloned.1.call-done = bf16[1536,1536]{1,0:T(8,128)(2,1)} async-done(((bf16[192,1536]{1,0:T(8,128)(2,1)}), bf16[1536,1536]{1,0:T(8,128)(2,1)}) %all-gather.18.cloned.1.call-update) | async-done | bytes 4718608 | tf_op jit(solution)/shard_map/all_gather | solution.py:89
  374.6 12.0 %fusion.46 = bf16[1024,1536]{1,0:T(8,128)(2,1)S(1)} fusion(f32[1024,1536]{1,0:T(8,128)} %fusion.91, f32[1536]{0:T(1024)S(1)} %fusion.83, bf16[1536,1536]{1,0:T(8,128)(2,1)} %all-gather.18.cloned.1.call-done, bf16[2048,1536]{1,0:T(8,128)(2,1)} %constant_dynamic-update-slice_fusion, s32[]{:T(128)S(6)} %select_n.39), kind=kOutput, calls=%fused_computation.58 | convolution fusion | flops 4864868352 | bytes 17307652 | tf_op jit(solution)/shard_map/td,sd->ts/dot_general | solution.py:160
  394.8 60.4 %reduce-scatter.13.cloned.1.call-done = bf16[256,1536]{1,0:T(8,128)(2,1)} async-done(((bf16[1024,1536]{1,0:T(8,128)(2,1)}), bf16[256,1536]{1,0:T(8,128)(2,1)}) %reduce-scatter.13.cloned.1.call-update) | async-done | bytes 786448 | tf_op jit(solution)/shard_map/reduce_scatter | solution.py:165
  461.2 63.4 %all-gather.20.cloned.1.call-done = bf16[1024,1536]{1,0:T(8,128)(2,1)} async-done(((bf16[256,1536]{1,0:T(8,128)(2,1)}), bf16[1024,1536]{1,0:T(8,128)(2,1)}) %all-gather.20.cloned.1.call-update) | async-done | bytes 3145744 | tf_op jit(solution)/shard_map/all_gather | solution.py:173
  529.1 33.0 %while.29 = (s32[]{:T(128)}, f32[1024,3,128]{0,2,1:T(8,128)S(1)}, f32[1024,3,128]{0,2,1:T(8,128)}, f32[2,512,3,128]{3,1,0,2:T(8,128)}, s32[2]{0:T(128)S(1)}, /*i...) while((s32[]{:T(128)}, f32[1024,3,128]{0,2,1:T(8,128)S(1)}, ...), condition=%wide.region_18.19_spmd.clone, body=%wide.region_16.18_spmd.clone.sunk | while | flops 2040593408 | bytes 91812304 | solution.py:208
  580.3 10.3 %convolution_convert_fusion.1 = bf16[1024,1536]{1,0:T(8,128)(2,1)} fusion(bf16[1536,1536]{1,0:T(8,128)(2,1)} %all-gather.18.cloned.1.call-done, f32[1024,1536]{1,0:T(8,128)} %fusion.91, f32[1536]{0:T(1024)S(1)} %fusion.83), kind=kOutput, calls=%fused_computation.62 | convolution fusion | flops 4849139712 | bytes 14161920 | tf_op jit(solution)/shard_map/dot_general | solution.py:147
  590.6 11.0 %fusion.51 = f32[1536,1536]{1,0:T(8,128)} fusion(bf16[2048,1536]{1,0:T(8,128)(2,1)} %constant_dynamic-update-slice_fusion, s32[]{:T(128)S(6)} %select_n.39, f32[1024,1536]{1,0:T(8,128)} %fusion.91, f32[1536]{0:T(1024)S(1)} %fusion.83), kind=kOutput, calls=%fused_computation.68 | convolution fusion | flops 4847566848 | bytes 18880516 | tf_op jit(solution)/shard_map/ts,td->sd/dot_general | solution.py:163
  601.7 10.4 %fusion.93 = f32[1536,1536]{1,0:T(8,128)} fusion(bf16[1024,1536]{1,0:T(8,128)(2,1)} %all-gather.14.cloned.1.call-done, bf16[1024,1536]{1,0:T(8,128)(2,1)} %copy-done.43), kind=kOutput, calls=%fused_computation.162 | convolution fusion | flops 4831838208 | bytes 15728640 | tf_op jit(solution)/shard_map/td,ts->ds/dot_general | solution.py:162
  627.3 12.0 %reduce-scatter.15.cloned.1.call-done = bf16[256,1536]{1,0:T(8,128)(2,1)} async-done(((bf16[1024,1536]{1,0:T(8,128)(2,1)}), bf16[256,1536]{1,0:T(8,128)(2,1)}) %reduce-scatter.15.cloned.1.call-update) | async-done | bytes 786448 | tf_op jit(solution)/shard_map/reduce_scatter | solution.py:226
  641.2 45.7 %all-reduce = (f32[1536]{0:T(1024)}, f32[1536]{0:T(1024)}, f32[1536]{0:T(1024)}, f32[1536]{0:T(1024)}) all-reduce(f32[1536]{0:T(1024)S(1)} %get-tuple-element.226, f32[1536]{0:T(1024)S(1)} %get-tuple-element.231, f32[1536]{0:T(1024)S(1)} %copy-done.28, f32[1536]{0:T(1024)S(1)} %copy-done.29), channel_id=1, replica_groups=mesh['dp'=8,'mp'=4] {'dp','mp'}, use_global_device_ids=true, to_apply=%region_23.24 | all-reduce | flops 6144 | bytes 49152 | tf_op jit(solution)/shard_map/psum | solution.py:234
  686.9 16.0 %reduce-scatter.11.cloned.1.call-done = bf16[256,1536]{1,0:T(8,128)(2,1)} async-done(((bf16[1024,1536]{1,0:T(8,128)(2,1)}), bf16[256,1536]{1,0:T(8,128)(2,1)}) %reduce-scatter.11.cloned.1.call-update) | async-done | bytes 786448 | tf_op jit(solution)/shard_map/reduce_scatter | solution.py:150
  706.7 76.8 %reduce-scatter.23.cloned.1.call-done = f32[192,1536]{1,0:T(8,128)} async-done(((f32[1536,1536]{1,0:T(8,128)}), f32[192,1536]{1,0:T(8,128)}) %reduce-scatter.23.cloned.1.call-update) | async-done | bytes 1179664 | tf_op jit(solution)/shard_map/reduce_scatter | solution.py:239
  783.5 80.6 %reduce-scatter.21.cloned.1.call-done = f32[192,1536]{1,0:T(8,128)} async-done(((f32[1536,1536]{1,0:T(8,128)}), f32[192,1536]{1,0:T(8,128)}) %reduce-scatter.21.cloned.1.call-update) | async-done | bytes 1179664 | tf_op jit(solution)/shard_map/reduce_scatter | solution.py:237
  864.0 46.3 %reduce-scatter.19.cloned.1.call-done = f32[48,1536]{1,0:T(8,128)} async-done(((f32[384,1536]{1,0:T(8,128)}), f32[48,1536]{1,0:T(8,128)}) %reduce-scatter.19.cloned.1.call-update) | async-done | bytes 294928 | tf_op jit(solution)/shard_map/reduce_scatter | solution.py:238
  910.4 69.9 %reduce-scatter.17.cloned.1.call-done = f32[192,3,384]{2,0,1:T(8,128)} async-done(((f32[1536,3,384]{2,0,1:T(8,128)}), f32[192,3,384]{2,0,1:T(8,128)}) %reduce-scatter.17.cloned.1.call-update) | async-done | bytes 884752 | tf_op jit(solution)/shard_map/reduce_scatter | solution.py:236
  (240 shorter events, 157.0 us)
Async XLA Ops:
  7.2 71.7 %all-gather.8.cloned.1.call-start = ((), (), s32[]{:S(2)}) async-start(), calls=%async_computation.8 | async-start | bytes 3932160 | tf_op jit(solution)/shard_map/all_gather | solution.py:104
  8.6 111.8 %copy-start.30 = (f32[256]{0:T(256)}, f32[256]{0:T(256)S(1)}, u32[]{:S(2)}) copy-start(f32[256]{0:T(256)S(1)} %broadcast_multiply_fusion.5) | copy-start | bytes 3076
  10.1 110.3 %copy-start.34 = (f32[256]{0:T(256)}, f32[256]{0:T(256)S(1)}, u32[]{:S(2)}) copy-start(f32[256]{0:T(256)S(1)} %add_rsqrt_fusion.1) | copy-start | bytes 3076
  12.5 100.9 %all-gather.10.cloned.1.call-start = ((), (), s32[]{:S(2)}) async-start(), calls=%async_computation.9 | async-start | bytes 3981312 | tf_op jit(solution)/shard_map/all_gather | solution.py:86
  13.2 138.9 %all-gather.12.cloned.1.call-start = ((), (), s32[]{:S(2)}) async-start(), calls=%async_computation.10 | async-start | bytes 1327104 | tf_op jit(solution)/shard_map/all_gather | solution.py:88
  14.0 203.6 %reduce-scatter.9.cloned.1.call-start = ((), (), s32[]{:S(2)}) async-start(), calls=%async_computation.11 | async-start | bytes 3932160 | tf_op jit(solution)/shard_map/reduce_scatter | solution.py:137
  157.2 153.9 %all-gather.16.cloned.1.call-start = ((), (), s32[]{:S(2)}) async-start(), calls=%async_computation.13 | async-start | bytes 5308416 | tf_op jit(solution)/shard_map/all_gather | solution.py:87
  157.7 177.8 %all-gather.14.cloned.1.call-start = ((), (), s32[]{:S(2)}) async-start(), calls=%async_computation.12 | async-start | bytes 3932160 | tf_op jit(solution)/shard_map/all_gather | solution.py:141
  219.1 238.7 %copy-start.26 = (f32[256]{0:T(256)}, f32[256]{0:T(256)S(1)}, u32[]{:S(2)}) copy-start(f32[256]{0:T(256)S(1)} %broadcast_multiply_fusion.4) | copy-start | bytes 3076
  220.6 237.1 %copy-start.32 = (f32[256]{0:T(256)}, f32[256]{0:T(256)S(1)}, u32[]{:S(2)}) copy-start(f32[256]{0:T(256)S(1)} %add_rsqrt_fusion) | copy-start | bytes 3076
  222.0 152.6 %all-gather.18.cloned.1.call-start = ((), (), s32[]{:S(2)}) async-start(), calls=%async_computation.14 | async-start | bytes 5308416 | tf_op jit(solution)/shard_map/all_gather | solution.py:89
  222.7 232.4 %reduce-scatter.13.cloned.1.call-start = ((), (), s32[]{:S(2)}) async-start(), calls=%async_computation.16 | async-start | bytes 3932160 | tf_op jit(solution)/shard_map/reduce_scatter | solution.py:165
  222.8 21.2 %collective-permute-start = (bf16[256,1536]{1,0:T(8,128)(2,1)}, bf16[256,1536]{1,0:T(8,128)(2,1)S(1)}, u32[]{:S(2)}, u32[]{:S(2)}) collective-permute-start(bf16[256,1536]{1,0:T(8,128)(2,1)} %param.17), channel_id=1, source_target_pairs={{0,1},{1,2},{2,3},{3,0},{4,5},{5,6},{6,7},{7,4},{8,9},{9,10},{10,1... | collective-permute-start | bytes 2359304 | tf_op jit(solution)/shard_map/ppermute | solution.py:156
  244.8 20.1 %collective-permute-start.1 = (bf16[256,1536]{1,0:T(8,128)(2,1)S(1)}, bf16[256,1536]{1,0:T(8,128)(2,1)}, u32[]{:S(2)}, u32[]{:S(2)}) collective-permute-start(bf16[256,1536]{1,0:T(8,128)(2,1)S(1)} %collective-permute-done), channel_id=1, source_target_pairs={{0,1},{1,2},{2,3},{3,0},{4,5},{5,6},{6,7},{7,4},{8,9},{9,10},{10,1... | collective-permute-start | bytes 2359304 | tf_op jit(solution)/shard_map/ppermute | solution.py:156
  265.0 34.0 %collective-permute-start.2 = (bf16[256,1536]{1,0:T(8,128)(2,1)}, bf16[256,1536]{1,0:T(8,128)(2,1)}, u32[]{:S(2)}, u32[]{:S(2)}) collective-permute-start(bf16[256,1536]{1,0:T(8,128)(2,1)} %collective-permute-done.1), channel_id=1, source_target_pairs={{0,1},{1,2},{2,3},{3,0},{4,5},{5,6},{6,7},{7,4},{8,9},{9,10},{10,1... | collective-permute-start | bytes 2359304 | tf_op jit(solution)/shard_map/ppermute | solution.py:156
  394.7 129.9 %all-gather.20.cloned.1.call-start = ((), (), s32[]{:S(2)}) async-start(), calls=%async_computation.17 | async-start | bytes 3932160 | tf_op jit(solution)/shard_map/all_gather | solution.py:173
  460.9 178.4 %reduce-scatter.15.cloned.1.call-start = ((), (), s32[]{:S(2)}) async-start(), calls=%async_computation.18 | async-start | bytes 3932160 | tf_op jit(solution)/shard_map/reduce_scatter | solution.py:226
  580.2 122.8 %reduce-scatter.11.cloned.1.call-start = ((), (), s32[]{:S(2)}) async-start(), calls=%async_computation.15 | async-start | bytes 3932160 | tf_op jit(solution)/shard_map/reduce_scatter | solution.py:150
  590.6 192.9 %reduce-scatter.23.cloned.1.call-start = ((), (), s32[]{:S(2)}) async-start(), calls=%async_computation.22 | async-start | bytes 10616832 | tf_op jit(solution)/shard_map/reduce_scatter | solution.py:239
  601.7 262.4 %reduce-scatter.21.cloned.1.call-start = ((), (), s32[]{:S(2)}) async-start(), calls=%async_computation.21 | async-start | bytes 10616832 | tf_op jit(solution)/shard_map/reduce_scatter | solution.py:237
  612.2 298.2 %reduce-scatter.19.cloned.1.call-start = ((), (), s32[]{:S(2)}) async-start(), calls=%async_computation.20 | async-start | bytes 2654208 | tf_op jit(solution)/shard_map/reduce_scatter | solution.py:238
  618.0 362.3 %reduce-scatter.17.cloned.1.call-start = ((), (), s32[]{:S(2)}) async-start(), calls=%async_computation.19 | async-start | bytes 7962624 | tf_op jit(solution)/shard_map/reduce_scatter | solution.py:236
  627.2 75.8 %copy-start.5 = (bf16[256,1536]{1,0:T(8,128)(2,1)S(1)}, bf16[256,1536]{1,0:T(8,128)(2,1)}, u32[]{:S(2)}) copy-start(bf16[256,1536]{1,0:T(8,128)(2,1)} %reduce-scatter.9.cloned.1.call-done) | copy-start | bytes 2359300
  627.2 75.8 %copy-start.7 = (bf16[256,1536]{1,0:T(8,128)(2,1)S(1)}, bf16[256,1536]{1,0:T(8,128)(2,1)}, u32[]{:S(2)}) copy-start(bf16[256,1536]{1,0:T(8,128)(2,1)} %param.17) | copy-start | bytes 2359300
  (44 other events, 1007.9 us)
Sparse Core Ops, SparseCore 0:
  12.6 66.1 all-gather.7
  80.7 32.6 all-gather.9
  115.3 24.0 all-gather.11
  157.3 60.2 reduce-scatter.8
  219.3 38.9 all-gather.15
  260.3 75.2 all-gather.13
  337.4 37.1 all-gather.17
  394.9 60.2 reduce-scatter.12
  461.0 63.5 all-gather.19
  580.3 58.8 reduce-scatter.14
  641.6 61.3 reduce-scatter.10
  706.9 76.5 reduce-scatter.22
  787.5 76.4 reduce-scatter.20
  867.8 42.4 reduce-scatter.18
  914.7 65.4 reduce-scatter.16
